TPU v7x, 32 devices: a whole 2x2x4 slice. The times are simulated.
32 devices in a mesh: grid: 8 (over y, x, core), pt: 4 (over z).
Axes of the slice: x: 2, y: 2, z: 4, core: 2. Of those that a mesh axis runs over, the one named last changes fastest.
Arguments:
- orbitals: bfloat16 [2048, 4096], P('grid'), may hold values from -0.875 to 0.875
- point_index: int32 [2048], P('pt'), may hold values from 0 to 4095, as said below
- factor_panels: float32 [2048, 1024], P('pt'), as said below
Outputs:
- solved: float32 [4096, 2048], P('grid', 'pt')
Inputs may be any that keep to these rules, and one draw needn't show every extreme that they name: `point_index`: all entries are different; 0 and 4095 are always among them. `factor_panels`: lower triangular in its global row and column indices, diagonal between 1.5 and 3.
All inputs are finite; a program needn't handle non-finite values.
Results may differ from a plain program's by a relative error of at most 0.0018.
Values may be sent and summed in bfloat16 or wider, within the bound.
A program may use at most 64 MiB of HBM per device.

v0:
```python
import jax
import jax.numpy as jnp
from jax import lax
from jax.sharding import PartitionSpec as P


def spread(x, axis, root):
    mine = lax.axis_index(axis) == root
    return lax.psum(jnp.where(mine, x, jnp.zeros_like(x)), axis)


def solve_panel(factor, targets):
    return lax.linalg.triangular_solve(
        factor, targets, left_side=False, lower=True, transpose_a=True
    )


def apply_factor(panel_round, factor):
    upper_part = factor.astype(jnp.bfloat16)
    lower_part = (factor - upper_part.astype(jnp.float32)).astype(jnp.bfloat16)
    dims = (((1,), (1,)), ((), ()))
    high_term = lax.dot_general(panel_round, upper_part, dims, preferred_element_type=jnp.float32)
    low_term = lax.dot_general(panel_round, lower_part, dims, preferred_element_type=jnp.float32)
    return high_term + low_term


def on_device(orbitals, point_index, factor_panels):
    own_bands, grid_rows = orbitals.shape
    grid_count = lax.axis_size("grid")
    rows_here = grid_rows // grid_count
    panel_cols = point_index.shape[0]
    at_points = jnp.take(orbitals, point_index, axis=1)
    point_orbs = lax.all_gather(at_points, "grid", axis=0, tiled=True)
    blocked = orbitals.reshape(own_bands, grid_count, rows_here)
    inner_sums = lax.dot_general(
        lax.all_to_all(blocked, "grid", split_axis=1, concat_axis=0, tiled=True)[:, 0, :],
        point_orbs,
        (((0,), (0,)), ((), ())),
        preferred_element_type=jnp.float32,
    )
    products = inner_sums * inner_sums
    rank_pt = lax.axis_index("pt")
    factor_first = factor_panels[:, 0:panel_cols]
    factor_second = factor_panels[:, panel_cols : 2 * panel_cols]
    first_solved = lax.cond(
        rank_pt == 0, lambda: solve_panel(factor_first, products), lambda: jnp.zeros_like(products)
    )
    first_round = spread(first_solved.astype(jnp.bfloat16), "pt", 0)
    left_over = lax.cond(
        rank_pt > 0, lambda: products - apply_factor(first_round, factor_first), lambda: products
    )
    second_solved = lax.cond(
        rank_pt == 1,
        lambda: solve_panel(factor_second, left_over),
        lambda: jnp.zeros_like(left_over),
    )
    second_round = spread(second_solved.astype(jnp.bfloat16), "pt", 1)
    trailing = lax.cond(
        rank_pt > 1,
        lambda: left_over - apply_factor(second_round, factor_second),
        lambda: left_over,
    )
    return jnp.where(rank_pt == 0, first_solved, jnp.where(rank_pt == 1, second_solved, trailing))


def solution(mesh):
    in_specs = (P("grid", None), P("pt"), P("pt", None))
    out_specs = P("grid", "pt")
    return jax.shard_map(
        on_device, mesh=mesh, in_specs=in_specs, out_specs=out_specs, check_vma=False
    )
```

profile of v0, /device:TPU:0, one launch (start us, length us, event | category | flops | bytes accessed | tf_op | source)
XLA Modules:
  0.0 292.4 jit_solution(4851775570383524236)
XLA Ops:
  7.9 4.1 %copy.26 = bf16[256,4096]{0,1:T(8,128)(2,1)} copy(bf16[256,4096]{1,0:T(8,128)(2,1)} %param.13) | data formatting | bytes 4194304 | tf_op args[0]
  12.0 3.4 %gather_fusion = bf16[512,256]{1,0:T(8,128)(2,1)S(1)} fusion(bf16[256,4096]{0,1:T(8,128)(2,1)} %copy.26, s32[1024]{0:T(1024)S(1)} %pad_clamp_fusion), kind=kCustom, calls=%fused_computation | custom fusion | bytes 526336 | tf_op jit(solution)/shard_map/jit(_take)/gather | solution.py:32
  16.3 5.2 %all-to-all-start = ((bf16[256,8,512]{0,2,1:T(8,128)(2,1)}), bf16[256,8,512]{0,2,1:T(8,128)(2,1)}, u32[]{:S(2)}, u32[]{:S(2)}) async-start(bf16[256,8,512]{0,2,1:T(8,128)(2,1)} %bitcast.13), calls=%async_computation | async-start | bytes 4194304 | tf_op jit(solution)/shard_map/all_to_all | solution.py:36
  23.3 31.2 %all-to-all-done = bf16[256,8,512]{0,2,1:T(8,128)(2,1)} async-done(((bf16[256,8,512]{0,2,1:T(8,128)(2,1)}), bf16[256,8,512]{0,2,1:T(8,128)(2,1)}, u32[]{:S(2)}, u32[]{:S(2)}) %all-to-all-start) | async-done | bytes 2097184 | tf_op jit(solution)/shard_map/all_to_all | solution.py:36
  54.5 3.9 %copy.28 = bf16[8,256,1,512]{3,1,0,2:T(8,128)(2,1)} copy(bf16[8,256,1,512]{1,3,0,2:T(8,128)(2,1)} %bitcast.15) | data formatting | bytes 4194304 | tf_op jit(solution)/shard_map/all_to_all | solution.py:36
  58.5 3.5 %fusion.50 = f32[512,512]{0,1:T(8,128)S(1)} fusion(bf16[2048,512]{0,1:T(8,128)(2,1)} %all-gather.2.cloned.1.call-done, bf16[2048,512]{1,0:T(8,128)(2,1)} %bitcast.89), kind=kOutput, calls=%fused_computation.80 | convolution fusion | flops 1074003968 | bytes 5242880 | tf_op jit(solution)/shard_map/dot_general | solution.py:35
  62.0 71.8 %conditional.4 = (f32[512,512]{1,0:T(8,128)}, bf16[512,512]{1,0:T(8,128)(2,1)}) conditional(s32[]{:T(128)} %convert_element_type.42, () %tuple.38, (f32[512,512]{1,0:T(8,128)S(1)}, f32[512,512]{0,1:T(8,128)S(1)}) %tuple.39), branch_computations={%region_0.1_spmd, %region_1.3_spmd} | conditional | flops 1010761728 | bytes 25428344 | solution.py:45
  63.1 11.3 %while.4 = (s32[]{:T(128)}, f32[512,512]{1,0:T(8,128)}, s32[4,2]{0,1:T(2,128)S(1)}, f32[4,128,128]{2,1,0:T(8,128)S(1)}, s32[]{:T(128)}) while((s32[]{:T(128)}, f32[512,512]{1,0:T(8,128)}, s32[4,2]{0,1:T(2,128)S(1)}, f32[4,128,128]{2,1,0:T(8,128)S(1)}, s32[]{:T(128)}) %tuple.92), condition=%wide.while_cond, body=%wide.while_body.sunk | while | flops 2 | bytes 131181 | solution.py:13
  63.8 2.2 bitcast_dynamic-update-slice_fusion.5
  66.6 2.2 bitcast_dynamic-update-slice_fusion.5
  69.4 2.2 bitcast_dynamic-update-slice_fusion.5
  72.3 2.1 bitcast_dynamic-update-slice_fusion.5
  74.4 39.9 %custom-call.4 = f32[4,128,128]{1,2,0:T(8,128)} custom-call(f32[4,128,128]{2,1,0:T(8,128)S(1)} %get-tuple-element.70), custom_call_target="InvertDiagBlocksLowerTriangular" | custom-call | tf_op jit(solution)/shard_map/cond/branch_1_fun/triangular_solve/custom-call.1 | solution.py:13
  120.0 2.0 convolution_subtract_fusion
  122.5 2.5 convolution_subtract_fusion.2
  127.0 2.0 copy.41
  129.1 2.2 pad_maximum_fusion
  131.2 2.5 copy.39
  133.8 1.9 broadcast_select_fusion.1
  135.7 35.0 %all-reduce.3.cloned.1.call-done = bf16[512,512]{1,0:T(8,128)(2,1)} async-done(((bf16[512,512]{1,0:T(8,128)(2,1)}), bf16[512,512]{1,0:T(8,128)(2,1)}) %all-reduce.3.cloned.1.call-update) | async-done | bytes 524304 | tf_op jit(solution)/shard_map/psum | solution.py:9
  170.8 2.8 conditional.5
  173.6 2.0 conditional.6
  176.4 107.0 %all-reduce.5.cloned.1.call-done = bf16[512,512]{1,0:T(8,128)(2,1)} async-done(((bf16[512,512]{1,0:T(8,128)(2,1)}), bf16[512,512]{1,0:T(8,128)(2,1)}) %all-reduce.5.cloned.1.call-update) | async-done | bytes 524304 | tf_op jit(solution)/shard_map/psum | solution.py:9
  283.4 2.5 select_select_fusion
  (48 shorter events, 21.2 us)
Async XLA Ops:
  6.5 51.9 %all-gather.2.cloned.1.call-start = ((), (), s32[]{:S(2)}) async-start(), calls=%async_computation.1 | async-start | bytes 2359296 | tf_op jit(solution)/shard_map/all_gather | solution.py:33
  16.3 38.2 %all-to-all-start = ((bf16[256,8,512]{0,2,1:T(8,128)(2,1)}), bf16[256,8,512]{0,2,1:T(8,128)(2,1)}, u32[]{:S(2)}, u32[]{:S(2)}) async-start(bf16[256,8,512]{0,2,1:T(8,128)(2,1)} %bitcast.13), calls=%async_computation | async-start | bytes 4194304 | tf_op jit(solution)/shard_map/all_to_all | solution.py:36
  21.5 149.3 %all-reduce.3.cloned.1.call-start = ((), (), s32[]{:S(2)}) async-start(), calls=%async_computation.2 | async-start | bytes 1048576 | tf_op jit(solution)/shard_map/psum | solution.py:9
  115.7 4.4 %copy-start.2 = (f32[512,512]{1,0:T(8,128)S(1)}, f32[512,512]{1,0:T(8,128)}, u32[]{:S(2)}) copy-start(f32[512,512]{1,0:T(8,128)} %copy.29) | copy-start | bytes 3145732 | tf_op jit(solution)/shard_map/cond
  115.7 6.4 %copy-start.7 = (f32[4,128,128]{1,2,0:T(8,128)S(1)}, f32[4,128,128]{1,2,0:T(8,128)}, u32[]{:S(2)}) copy-start(f32[4,128,128]{1,2,0:T(8,128)} %custom-call.4) | copy-start | bytes 786436 | tf_op jit(solution)/shard_map/cond
  120.0 5.4 %copy-start.1 = (f32[512,128]{0,1:T(8,128)}, f32[512,128]{0,1:T(8,128)S(1)}, u32[]{:S(2)}) copy-start(f32[512,128]{0,1:T(8,128)S(1)} %fusion.25) | copy-start | bytes 786436 | tf_op jit(solution)/shard_map/cond
  122.5 2.9 %copy-start.3 = (f32[512,128]{0,1:T(8,128)}, f32[512,128]{0,1:T(8,128)S(1)}, u32[]{:S(2)}) copy-start(f32[512,128]{0,1:T(8,128)S(1)} %fusion.24) | copy-start | bytes 786436 | tf_op jit(solution)/shard_map/cond
  125.4 0.7 copy-start.5
  135.7 147.7 %all-reduce.5.cloned.1.call-start = ((), (), s32[]{:S(2)}) async-start(), calls=%async_computation.3 | async-start | bytes 1048576 | tf_op jit(solution)/shard_map/psum | solution.py:9
  170.8 1.0 copy-start
Sparse Core Ops, SparseCore 0:
  16.4 42.0 all-gather.1
  135.8 34.9 all-reduce.2
  176.5 106.7 all-reduce.4
where the time goes:
time: 293 us; the launch traced here: 292 us
  waiting for transfers between devices  173 us (59%)
  other arithmetic  51.6 us (18%)
  local copies, waits for them, and re-layouts  35.5 us (12%)
  between operations  13.2 us (5%)
  matrix products  13.1 us (4%)
  starting transfers between devices  5.29 us (2%)
    psum x2, waiting for transfers between devices, spread(): return lax.psum(jnp.where(mine, x, jnp.zeros_like(x)), axis)  142 us
    another operation x5, other arithmetic, solve_panel(): lax.linalg.triangular_solve(factor, targets, left_side=False, lower=True,...  43.3 us
    all_to_all x1, waiting for transfers between devices, on_device(): lax.all_to_all(blocked, 'grid', split_axis=1, concat_axis=0, tiled=True)  31.2 us
    another operation x12, local copies, waits for them, and re-layouts, solve_panel(): lax.linalg.triangular_solve(factor, targets, left_side=False, lower=True,...  11.2 us
    another operation x7, matrix products, solve_panel(): lax.linalg.triangular_solve(factor, targets, left_side=False, lower=True,...  9.67 us
  transfers between devices with their start and end apart: 4, of which 3 were waited for; matrix products, arithmetic and copies ran while one was open for 2% of the time, Pallas kernels for 0%

commit v1 on v0

--- a/solution.py
+++ b/solution.py
@@ -6,7 +6,7 @@
 
 def spread(x, axis, root):
     mine = lax.axis_index(axis) == root
-    return lax.psum(jnp.where(mine, x, jnp.zeros_like(x)), axis)
+    return jnp.sum(lax.all_gather(jnp.where(mine, x, jnp.zeros_like(x)), axis), axis=0)
 
 
 def solve_panel(factor, targets):

time: 293 us -> 310 us (1.058)
  waiting for transfers between devices: 173 us -> 189 us
    all_gather x0 -> x2, waiting for transfers between devices: none -> 158 us  [spread(): lax.all_gather(jnp.where(mine, x, jnp.zeros_like(x)), axis)]
    psum x2 -> x0, waiting for transfers between devices: 142 us -> none  [spread(): return lax.psum(jnp.where(mine, x, jnp.zeros_like(x)), axis)]
  transfers between devices with their start and end apart: 4 -> 4, of which waited for: 3 -> 4; matrix products, arithmetic and copies ran while one was open for 2% -> 2% of each run, Pallas kernels for 0% -> 0%
where the time goes in v1:
time: 310 us; the launch traced here: 309 us
  waiting for transfers between devices  189 us (61%)
  other arithmetic  51.6 us (17%)
  local copies, waits for them, and re-layouts  35.8 us (12%)
  between operations  13.2 us (4%)
  matrix products  13.1 us (4%)
  starting transfers between devices  5.29 us (2%)
    all_gather x2, waiting for transfers between devices, spread(): lax.all_gather(jnp.where(mine, x, jnp.zeros_like(x)), axis)  158 us
    another operation x5, other arithmetic, solve_panel(): lax.linalg.triangular_solve(factor, targets, left_side=False, lower=True,...  43.3 us
    all_to_all x1, waiting for transfers between devices, on_device(): lax.all_to_all(blocked, 'grid', split_axis=1, concat_axis=0, tiled=True)  31.2 us
    another operation x12, local copies, waits for them, and re-layouts, solve_panel(): lax.linalg.triangular_solve(factor, targets, left_side=False, lower=True,...  11.6 us
    another operation x7, matrix products, solve_panel(): lax.linalg.triangular_solve(factor, targets, left_side=False, lower=True,...  9.67 us
  transfers between devices with their start and end apart: 4, of which 4 were waited for; matrix products, arithmetic and copies ran while one was open for 2% of the time, Pallas kernels for 0%

profile of v1, /device:TPU:0, one launch (start us, length us, event | category | flops | bytes accessed | tf_op | source)
XLA Modules:
  0.0 308.5 jit_solution(2465836357052344138)
XLA Ops:
  7.9 4.1 %copy.20 = bf16[256,4096]{0,1:T(8,128)(2,1)} copy(bf16[256,4096]{1,0:T(8,128)(2,1)} %param.13) | data formatting | bytes 4194304 | tf_op args[0]
  12.0 3.4 %gather_fusion = bf16[512,256]{1,0:T(8,128)(2,1)S(1)} fusion(bf16[256,4096]{0,1:T(8,128)(2,1)} %copy.20, s32[1024]{0:T(1024)S(1)} %pad_clamp_fusion), kind=kCustom, calls=%fused_computation | custom fusion | bytes 526336 | tf_op jit(solution)/shard_map/jit(_take)/gather | solution.py:32
  16.3 5.2 %all-to-all-start = ((bf16[256,8,512]{0,2,1:T(8,128)(2,1)}), bf16[256,8,512]{0,2,1:T(8,128)(2,1)}, u32[]{:S(2)}, u32[]{:S(2)}) async-start(bf16[256,8,512]{0,2,1:T(8,128)(2,1)} %bitcast.11), calls=%async_computation | async-start | bytes 4194304 | tf_op jit(solution)/shard_map/all_to_all | solution.py:36
  23.3 31.2 %all-to-all-done = bf16[256,8,512]{0,2,1:T(8,128)(2,1)} async-done(((bf16[256,8,512]{0,2,1:T(8,128)(2,1)}), bf16[256,8,512]{0,2,1:T(8,128)(2,1)}, u32[]{:S(2)}, u32[]{:S(2)}) %all-to-all-start) | async-done | bytes 2097184 | tf_op jit(solution)/shard_map/all_to_all | solution.py:36
  54.5 3.9 %copy.22 = bf16[8,256,1,512]{3,1,0,2:T(8,128)(2,1)} copy(bf16[8,256,1,512]{1,3,0,2:T(8,128)(2,1)} %bitcast.13) | data formatting | bytes 4194304 | tf_op jit(solution)/shard_map/all_to_all | solution.py:36
  58.5 3.5 %fusion.48 = f32[512,512]{0,1:T(8,128)S(1)} fusion(bf16[2048,512]{0,1:T(8,128)(2,1)} %all-gather.6.cloned.1.call-done, bf16[2048,512]{1,0:T(8,128)(2,1)} %bitcast.81), kind=kOutput, calls=%fused_computation.78 | convolution fusion | flops 1074003968 | bytes 5242880 | tf_op jit(solution)/shard_map/dot_general | solution.py:35
  61.9 72.2 %conditional.4 = (f32[512,512]{1,0:T(8,128)}, bf16[512,512]{1,0:T(8,128)(2,1)}) conditional(s32[]{:T(128)} %convert_element_type.46, () %tuple.38, (f32[512,512]{1,0:T(8,128)S(1)}, f32[512,512]{0,1:T(8,128)S(1)}) %tuple.39), branch_computations={%region_0.1_spmd, %region_1.3_spmd} | conditional | flops 1010761728 | bytes 25428344 | solution.py:45
  63.1 11.7 %while.4 = (s32[]{:T(128)}, f32[512,512]{1,0:T(8,128)}, s32[4,2]{0,1:T(2,128)S(1)}, f32[4,128,128]{2,1,0:T(8,128)S(1)}, s32[]{:T(128)}) while((s32[]{:T(128)}, f32[512,512]{1,0:T(8,128)}, s32[4,2]{0,1:T(2,128)S(1)}, f32[4,128,128]{2,1,0:T(8,128)S(1)}, s32[]{:T(128)}) %tuple.92), condition=%wide.while_cond, body=%wide.while_body.sunk | while | flops 2 | bytes 131181 | solution.py:13
  63.8 2.3 bitcast_dynamic-update-slice_fusion.5
  66.7 2.3 bitcast_dynamic-update-slice_fusion.5
  69.6 2.3 bitcast_dynamic-update-slice_fusion.5
  72.6 2.2 bitcast_dynamic-update-slice_fusion.5
  74.8 39.9 %custom-call.4 = f32[4,128,128]{1,2,0:T(8,128)} custom-call(f32[4,128,128]{2,1,0:T(8,128)S(1)} %get-tuple-element.74), custom_call_target="InvertDiagBlocksLowerTriangular" | custom-call | tf_op jit(solution)/shard_map/cond/branch_1_fun/triangular_solve/custom-call.1 | solution.py:13
  120.4 2.0 convolution_subtract_fusion
  122.9 2.5 convolution_subtract_fusion.2
  127.4 2.1 copy.33
  129.4 2.2 pad_maximum_fusion
  131.6 2.5 copy.31
  134.1 1.9 broadcast_select_fusion.1
  136.1 42.2 %all-gather.8.cloned.1.call-done = bf16[2048,512]{1,0:T(8,128)(2,1)} async-done(((bf16[512,512]{1,0:T(8,128)(2,1)}), bf16[2048,512]{1,0:T(8,128)(2,1)}) %all-gather.8.cloned.1.call-update) | async-done | bytes 2097168 | tf_op jit(solution)/shard_map/all_gather | solution.py:9
  178.3 2.7 conditional.5
  181.0 2.0 conditional.6
  183.9 115.6 %all-gather.10.cloned.1.call-done = bf16[2048,512]{1,0:T(8,128)(2,1)} async-done(((bf16[512,512]{1,0:T(8,128)(2,1)}), bf16[2048,512]{1,0:T(8,128)(2,1)}) %all-gather.10.cloned.1.call-update) | async-done | bytes 2097168 | tf_op jit(solution)/shard_map/all_gather | solution.py:9
  299.5 2.5 select_select_fusion
  (48 shorter events, 21.3 us)
Async XLA Ops:
  6.5 51.9 %all-gather.6.cloned.1.call-start = ((), (), s32[]{:S(2)}) async-start(), calls=%async_computation.1 | async-start | bytes 2359296 | tf_op jit(solution)/shard_map/all_gather | solution.py:33
  16.3 38.2 %all-to-all-start = ((bf16[256,8,512]{0,2,1:T(8,128)(2,1)}), bf16[256,8,512]{0,2,1:T(8,128)(2,1)}, u32[]{:S(2)}, u32[]{:S(2)}) async-start(bf16[256,8,512]{0,2,1:T(8,128)(2,1)} %bitcast.11), calls=%async_computation | async-start | bytes 4194304 | tf_op jit(solution)/shard_map/all_to_all | solution.py:36
  21.5 156.8 %all-gather.8.cloned.1.call-start = ((), (), s32[]{:S(2)}) async-start(), calls=%async_computation.2 | async-start | bytes 2621440 | tf_op jit(solution)/shard_map/all_gather | solution.py:9
  116.0 4.4 %copy-start.2 = (f32[512,512]{1,0:T(8,128)S(1)}, f32[512,512]{1,0:T(8,128)}, u32[]{:S(2)}) copy-start(f32[512,512]{1,0:T(8,128)} %copy.23) | copy-start | bytes 3145732 | tf_op jit(solution)/shard_map/cond
  116.0 6.4 %copy-start.6 = (f32[4,128,128]{1,2,0:T(8,128)S(1)}, f32[4,128,128]{1,2,0:T(8,128)}, u32[]{:S(2)}) copy-start(f32[4,128,128]{1,2,0:T(8,128)} %custom-call.4) | copy-start | bytes 786436 | tf_op jit(solution)/shard_map/cond
  120.4 5.4 %copy-start.1 = (f32[512,128]{0,1:T(8,128)}, f32[512,128]{0,1:T(8,128)S(1)}, u32[]{:S(2)}) copy-start(f32[512,128]{0,1:T(8,128)S(1)} %fusion.23) | copy-start | bytes 786436 | tf_op jit(solution)/shard_map/cond
  122.8 2.9 copy-start.3
  125.8 0.7 copy-start.5
  136.0 163.4 %all-gather.10.cloned.1.call-start = ((), (), s32[]{:S(2)}) async-start(), calls=%async_computation.3 | async-start | bytes 2621440 | tf_op jit(solution)/shard_map/all_gather | solution.py:9
  178.3 1.0 copy-start
Sparse Core Ops, SparseCore 0:
  16.4 42.0 all-gather.5
  136.2 42.0 all-gather.7
  184.0 115.4 all-gather.9

commit v2 on v0

--- a/solution.py
+++ b/solution.py
@@ -33,7 +33,12 @@
     point_orbs = lax.all_gather(at_points, "grid", axis=0, tiled=True)
     blocked = orbitals.reshape(own_bands, grid_count, rows_here)
     inner_sums = lax.dot_general(
-        lax.all_to_all(blocked, "grid", split_axis=1, concat_axis=0, tiled=True)[:, 0, :],
+        jnp.concatenate(
+            lax.all_to_all(
+                jnp.stack(jnp.split(blocked, lax.axis_size("grid"), axis=1)), "grid", 0, 0
+            ),
+            axis=0,
+        )[:, 0, :],
         point_orbs,
         (((0,), (0,)), ((), ())),
         preferred_element_type=jnp.float32,

time: 293 us -> 292 us (level)
    unnamed x1 -> x8, local copies, waits for them, and re-layouts: 4.08 us -> 8.36 us
  transfers between devices with their start and end apart: 4 -> 4, of which waited for: 3 -> 3; matrix products, arithmetic and copies ran while one was open for 2% -> 4% of each run, Pallas kernels for 0% -> 0%
where the time goes in v2:
time: 292 us
  waiting for transfers between devices  173 us (59%)
  other arithmetic  51.6 us (18%)
  local copies, waits for them, and re-layouts  35.5 us (12%)
  between operations  13.2 us (5%)
  matrix products  12.9 us (4%)
  starting transfers between devices  5.28 us (2%)
    psum x2, waiting for transfers between devices, spread(): return lax.psum(jnp.where(mine, x, jnp.zeros_like(x)), axis)  141 us
    another operation x5, other arithmetic, solve_panel(): lax.linalg.triangular_solve(factor, targets, left_side=False, lower=True,...  43.2 us
    all_to_all x1, waiting for transfers between devices, on_device(): lax.all_to_all(jnp.stack(jnp.split(blocked, lax.axis_size('grid'), axis=1...  32.1 us
    another operation x12, local copies, waits for them, and re-layouts, solve_panel(): lax.linalg.triangular_solve(factor, targets, left_side=False, lower=True,...  11.5 us
    another operation x7, matrix products, solve_panel(): lax.linalg.triangular_solve(factor, targets, left_side=False, lower=True,...  9.36 us
    unnamed x8, local copies, waits for them, and re-layouts  8.36 us
  transfers between devices with their start and end apart: 4, of which 3 were waited for; matrix products, arithmetic and copies ran while one was open for 4% of the time, Pallas kernels for 0%

profile of v2, /device:TPU:0, one launch (start us, length us, event | category | flops | bytes accessed | tf_op | source)
XLA Modules:
  0.0 291.6 jit_solution(16674518785787383356)
XLA Ops:
  7.9 3.3 %copy.37 = bf16[256,4096]{0,1:T(8,128)(2,1)S(1)} copy(bf16[256,4096]{1,0:T(8,128)(2,1)} %param.13) | data formatting | bytes 4194304 | tf_op args[0]
  11.2 2.0 gather_fusion
  19.8 5.2 %all-to-all-start = ((bf16[8,256,1,512]{1,3,2,0:T(8,128)(2,1)}), bf16[8,256,1,512]{1,3,2,0:T(8,128)(2,1)}, u32[]{:S(2)}, u32[]{:S(2)}) async-start(bf16[8,256,1,512]{1,3,2,0:T(8,128)(2,1)} %fusion.50), calls=%async_computation | async-start | bytes 4194304 | tf_op jit(solution)/shard_map/all_to_all | solution.py:37
  25.1 1.7 fusion.60
  26.8 32.1 %all-to-all-done = bf16[8,256,1,512]{1,3,2,0:T(8,128)(2,1)} async-done(((bf16[8,256,1,512]{1,3,2,0:T(8,128)(2,1)}), bf16[8,256,1,512]{1,3,2,0:T(8,128)(2,1)}, u32[]{:S(2)}, u32[]{:S(2)}) %all-to-all-start) | async-done | bytes 2097184 | tf_op jit(solution)/shard_map/all_to_all | solution.py:37
  58.9 3.9 %copy.40 = bf16[8,256,1,512]{3,1,0,2:T(8,128)(2,1)} copy(bf16[8,256,1,512]{1,3,2,0:T(8,128)(2,1)} %all-to-all-done) | data formatting | bytes 4194304 | tf_op jit(solution)/shard_map/all_to_all | solution.py:37
  62.8 3.5 %convolution_multiply_fusion = f32[512,512]{1,0:T(8,128)S(1)} fusion(bf16[2048,512]{1,0:T(8,128)(2,1)} %bitcast.124, bf16[2048,512]{0,1:T(8,128)(2,1)} %all-gather.2.cloned.1.call-done), kind=kOutput, calls=%fused_computation.79 | convolution fusion | flops 1074003968 | bytes 5242880 | tf_op jit(solution)/shard_map/dot_general | solution.py:35
  66.4 70.5 %conditional.4 = (f32[512,512]{1,0:T(8,128)}, bf16[512,512]{1,0:T(8,128)(2,1)}) conditional(s32[]{:T(128)} %convert_element_type.42, () %tuple.38, (f32[512,512]{1,0:T(8,128)S(1)}, f32[512,512]{1,0:T(8,128)S(1)}) %tuple.39), branch_computations={%region_0.1_spmd, %region_1.3_spmd} | conditional | flops 1010761728 | bytes 19136860 | solution.py:50
  67.5 11.6 %while.4 = (s32[]{:T(128)}, f32[512,512]{1,0:T(8,128)}, s32[4,2]{0,1:T(2,128)S(1)}, f32[4,128,128]{2,1,0:T(8,128)S(1)}, s32[]{:T(128)}) while((s32[]{:T(128)}, f32[512,512]{1,0:T(8,128)}, s32[4,2]{0,1:T(2,128)S(1)}, f32[4,128,128]{2,1,0:T(8,128)S(1)}, s32[]{:T(128)}) %tuple.85), condition=%wide.while_cond, body=%wide.while_body.sunk | while | flops 2 | bytes 131181 | solution.py:13
  68.1 2.2 bitcast_dynamic-update-slice_fusion.5
  71.1 2.2 bitcast_dynamic-update-slice_fusion.5
  74.0 2.2 bitcast_dynamic-update-slice_fusion.5
  76.9 2.2 bitcast_dynamic-update-slice_fusion.5
  79.1 39.9 %custom-call.4 = f32[4,128,128]{1,2,0:T(8,128)} custom-call(f32[4,128,128]{2,1,0:T(8,128)S(1)} %get-tuple-element.70), custom_call_target="InvertDiagBlocksLowerTriangular" | custom-call | tf_op jit(solution)/shard_map/cond/branch_1_fun/triangular_solve/custom-call.1 | solution.py:13
  123.1 2.0 convolution_subtract_fusion
  125.5 2.5 convolution_subtract_fusion.2
  130.1 2.1 copy.52
  132.1 2.2 pad_maximum_fusion
  134.3 2.5 copy.50
  136.8 1.9 broadcast_select_fusion.1
  138.8 35.2 %all-reduce.3.cloned.1.call-done = bf16[512,512]{1,0:T(8,128)(2,1)} async-done(((bf16[512,512]{1,0:T(8,128)(2,1)}), bf16[512,512]{1,0:T(8,128)(2,1)}) %all-reduce.3.cloned.1.call-update) | async-done | bytes 524304 | tf_op jit(solution)/shard_map/psum | solution.py:9
  174.0 2.0 conditional.6
  176.9 105.6 %all-reduce.5.cloned.1.call-done = bf16[512,512]{1,0:T(8,128)(2,1)} async-done(((bf16[512,512]{1,0:T(8,128)(2,1)}), bf16[512,512]{1,0:T(8,128)(2,1)}) %all-reduce.5.cloned.1.call-update) | async-done | bytes 524304 | tf_op jit(solution)/shard_map/psum | solution.py:9
  282.5 2.5 select_select_fusion
  (50 shorter events, 21.2 us)
Async XLA Ops:
  6.5 56.3 %all-gather.2.cloned.1.call-start = ((), (), s32[]{:S(2)}) async-start(), calls=%async_computation.1 | async-start | bytes 2359296 | tf_op jit(solution)/shard_map/all_gather | solution.py:33
  19.8 39.1 %all-to-all-start = ((bf16[8,256,1,512]{1,3,2,0:T(8,128)(2,1)}), bf16[8,256,1,512]{1,3,2,0:T(8,128)(2,1)}, u32[]{:S(2)}, u32[]{:S(2)}) async-start(bf16[8,256,1,512]{1,3,2,0:T(8,128)(2,1)} %fusion.50), calls=%async_computation | async-start | bytes 4194304 | tf_op jit(solution)/shard_map/all_to_all | solution.py:37
  25.0 149.0 %all-reduce.3.cloned.1.call-start = ((), (), s32[]{:S(2)}) async-start(), calls=%async_computation.2 | async-start | bytes 1048576 | tf_op jit(solution)/shard_map/psum | solution.py:9
  119.0 6.1 %copy-start.6 = (f32[4,128,128]{1,2,0:T(8,128)S(1)}, f32[4,128,128]{1,2,0:T(8,128)}, u32[]{:S(2)}) copy-start(f32[4,128,128]{1,2,0:T(8,128)} %custom-call.4) | copy-start | bytes 786436 | tf_op jit(solution)/shard_map/cond
  123.1 5.4 %copy-start = (f32[512,128]{0,1:T(8,128)}, f32[512,128]{0,1:T(8,128)S(1)}, u32[]{:S(2)}) copy-start(f32[512,128]{0,1:T(8,128)S(1)} %fusion.25) | copy-start | bytes 786436 | tf_op jit(solution)/shard_map/cond
  125.5 3.0 %copy-start.1 = (f32[512,128]{0,1:T(8,128)}, f32[512,128]{0,1:T(8,128)S(1)}, u32[]{:S(2)}) copy-start(f32[512,128]{0,1:T(8,128)S(1)} %fusion.24) | copy-start | bytes 786436 | tf_op jit(solution)/shard_map/cond
  128.5 0.7 copy-start.3
  138.8 143.7 %all-reduce.5.cloned.1.call-start = ((), (), s32[]{:S(2)}) async-start(), calls=%async_computation.3 | async-start | bytes 1048576 | tf_op jit(solution)/shard_map/psum | solution.py:9
Sparse Core Ops, SparseCore 0:
  14.1 42.8 all-gather.1
  138.9 35.1 all-reduce.2
  177.0 105.4 all-reduce.4
